TPU v7x, 512 devices: a whole 4x8x8 slice. The times are simulated.
512 devices in a mesh: blk: 16 (over x, y_lo), neg: 32 (over z, y_hi, core).
Axes of the slice: x: 4, y: 8 (y_hi: 2, y_lo: 4; y = y_hi * 4 + y_lo), z: 8, core: 2. Of those that a mesh axis runs over, the one named last changes fastest.
Arguments:
- queries: bfloat16 [65536, 768], P(('blk', 'neg')), may hold values from -12 to 12
- passages: bfloat16 [65536, 768], P(('blk', 'neg')), may hold values from -3 to 3
- positive: int32 [65536], P(('blk', 'neg')), may hold values from 0 to 127
- hard_owner: int32 [16, 4], P('blk'), may hold values from 0 to 31
- hard_block: int32 [16, 4], P('blk'), may hold values from 0 to 7
- hard_pick: int32 [1024, 2], P(('blk', 'neg')), may hold values from 0 to 3, all different within a row
Outputs:
- loss: float32 [], replicated
- query_grad: bfloat16 [65536, 768], P(('blk', 'neg'))
- passage_grad: bfloat16 [65536, 768], P(('blk', 'neg'))
Inputs may be any that keep to these rules, and one draw needn't show every extreme that they name: `hard_pick`: the 2 blocks of a query group differ.
All inputs are finite; a program needn't handle non-finite values.
Results may differ from a plain program's by a relative error of at most 0.014.
Values may be sent and summed in bfloat16 or wider, within the bound.
A program may use at most 64 MiB of HBM per device.

v0:
```python
import jax
import jax.numpy as jnp
from jax import lax
from jax.sharding import PartitionSpec as P

STEPS = 1
H = 4
HB = 16
GQ = 64


def from_behind(block, axis, distance):
    devices = range(lax.axis_size(axis))
    route = [((i - distance) % len(devices), i) for i in devices]
    return lax.ppermute(block, axis, route)


def from_root(value, axis, source):
    kept = jnp.where(lax.axis_index(axis) == source, value, 0).astype(value.dtype)
    return lax.psum(kept, axis)


def contract_rows(left, right):
    return lax.dot_general(
        left, right, (((0,), (0,)), ((), ())), preferred_element_type=jnp.float32
    )


def body(queries, passages, positive, hard_owner, hard_block, hard_pick):
    rows, width = passages.shape
    scale = width ** (-0.5)
    slots = rows // HB
    owner = hard_owner[0]
    block = hard_block[0]
    member = lax.axis_index("neg")
    slot_view = passages.reshape(slots, HB, width)
    cycle = [passages]
    moving = passages
    moving = from_behind(moving, "blk", 1)
    cycle.append(moving)
    select = ((owner[:, None] == member) & (block[:, None] == jnp.arange(slots)[None, :])).astype(
        jnp.float32
    )

    def fetch(index, stack):
        piece = lax.dynamic_index_in_dim(slot_view, block[index], 0, keepdims=False)
        got = from_root(piece, "neg", owner[index])
        return lax.dynamic_update_index_in_dim(stack, got, index, 0)

    hard = lax.fori_loop(0, H, fetch, jnp.zeros((H, HB, width), jnp.bfloat16))
    cycle_width = (STEPS + 1) * rows
    cand = jnp.concatenate(cycle + [hard.reshape(H * HB, width)], axis=0)
    scores = jnp.dot(queries, cand.T, preferred_element_type=jnp.float32) * scale
    allowed = jnp.any(hard_pick[:, :, None] == jnp.arange(H)[None, None, :], axis=1)
    hard_mask = jnp.repeat(jnp.repeat(allowed, GQ, axis=0), HB, axis=1)
    mask = jnp.concatenate([jnp.ones((rows, cycle_width), bool), hard_mask], axis=1)
    scores = jnp.where(mask, scores, -jnp.inf)
    top = jnp.max(scores, axis=1)
    lse = top + jnp.log(jnp.sum(jnp.exp(scores - top[:, None]), axis=1))
    onehot = jnp.arange(cand.shape[0])[None, :] == positive[:, None]
    spos = jnp.sum(jnp.where(onehot, scores, 0.0), axis=1)
    local_loss = jnp.sum(lse - spos)
    loss = lax.psum(local_loss, ("blk", "neg")) / (
        rows * lax.axis_size("blk") * lax.axis_size("neg")
    )
    grad_s = (jnp.exp(scores - lse[:, None]) - onehot.astype(jnp.float32)).astype(jnp.bfloat16)
    query_grad = (jnp.dot(grad_s, cand, preferred_element_type=jnp.float32) * scale).astype(
        jnp.bfloat16
    )
    own_grad = contract_rows(grad_s[:, :rows], queries) * scale
    hard_part = contract_rows(grad_s[:, cycle_width:], queries) * scale
    cycle_grad = contract_rows(grad_s[:, rows:cycle_width], queries) * scale
    carried = cycle_grad
    carried = from_behind(carried.astype(jnp.bfloat16), "blk", -1).astype(carried.dtype)
    shared_total = lax.psum(hard_part.reshape(H, HB, width).astype(jnp.bfloat16), "neg").astype(
        jnp.float32
    )
    returned = jnp.einsum("hb,hrd->brd", select, shared_total, precision=lax.Precision.HIGHEST)
    passage_grad = (own_grad + carried + returned.reshape(rows, width)).astype(jnp.bfloat16)
    return (loss, query_grad, passage_grad)


def solution(mesh):
    placed = (
        P(("blk", "neg"), None),
        P(("blk", "neg"), None),
        P(("blk", "neg")),
        P("blk", None),
        P("blk", None),
        P(("blk", "neg"), None),
    )
    return jax.shard_map(
        body,
        mesh=mesh,
        in_specs=placed,
        out_specs=(P(), P(("blk", "neg"), None), P(("blk", "neg"), None)),
        check_vma=False,
    )
```

profile of v0, /device:TPU:1, one launch (start us, length us, event | category | flops | bytes accessed | tf_op | source)
XLA Modules:
  0.0 1033.1 jit_solution(10842228640799932775)
XLA Ops:
  7.2 0.0 copy-start
  7.2 0.0 all-reduce.3.cloned.1.call-start
  7.2 4.2 collective-permute-start
  11.4 0.0 copy-start.3
  11.4 0.0 copy-start.5
  11.4 0.6 copy-done.3
  12.1 0.0 copy-done.5
  12.1 691.3 %while.15 = (s32[]{:T(128)}, bf16[4,16,768]{2,1,0:T(8,128)(2,1)S(1)}, s32[4]{0:T(128)S(1)}, s32[4]{0:T(128)S(1)}, bf16[8,16,768]{2,1,0:T(8,128)(2,1)}, /*index=5*/s32[]{:T(128)}, s32[]{:T(128)}, s32[]{:T(128)}, u32[]{:T(128)}) while((s32[]{:T(128)}, bf16[4,16,768]{2,1,0:T(8,128)(2,1)S(1)}, s32[4]{0:T(128)S(1)}, s32[4]{0:T(128)S(1)}, ...), condition=%wide.region_3.4_spmd, body=%wide.region_1.0_spmd.sunk | while | flops 24584 | bytes 147653 | solution.py:50
  12.1 0.6 dynamic_slice.36
  14.6 0.6 dynamic_slice.37
  15.9 0.7 dynamic-slice_select_fusion.2
  16.6 172.2 %psum.31 = bf16[1,16,768]{2,1,0:T(8,128)(2,1)S(1)} all-reduce(bf16[1,16,768]{2,1,0:T(8,128)(2,1)S(1)} %dynamic-slice_select_fusion.2), channel_id=1, replica_groups=mesh['blk'=16,'neg'=32] {'neg'}, use_global_device_ids=true, to_apply=%region_2.2 | all-reduce | flops 12288 | bytes 49152 | tf_op jit(solution)/shard_map/while/body/eval_jaxpr/psum | solution.py:20
  188.8 0.6 dynamic_slice.36
  191.3 0.6 dynamic_slice.37
  192.5 0.7 dynamic-slice_select_fusion.2
  193.3 167.0 %psum.31 = bf16[1,16,768]{2,1,0:T(8,128)(2,1)S(1)} all-reduce(bf16[1,16,768]{2,1,0:T(8,128)(2,1)S(1)} %dynamic-slice_select_fusion.2), channel_id=1, replica_groups=mesh['blk'=16,'neg'=32] {'neg'}, use_global_device_ids=true, to_apply=%region_2.2 | all-reduce | flops 12288 | bytes 49152 | tf_op jit(solution)/shard_map/while/body/eval_jaxpr/psum | solution.py:20
  360.3 0.6 dynamic_slice.36
  362.9 0.6 dynamic_slice.37
  364.1 0.7 dynamic-slice_select_fusion.2
  364.8 167.0 %psum.31 = bf16[1,16,768]{2,1,0:T(8,128)(2,1)S(1)} all-reduce(bf16[1,16,768]{2,1,0:T(8,128)(2,1)S(1)} %dynamic-slice_select_fusion.2), channel_id=1, replica_groups=mesh['blk'=16,'neg'=32] {'neg'}, use_global_device_ids=true, to_apply=%region_2.2 | all-reduce | flops 12288 | bytes 49152 | tf_op jit(solution)/shard_map/while/body/eval_jaxpr/psum | solution.py:20
  531.9 0.6 dynamic_slice.36
  534.4 0.6 dynamic_slice.37
  535.6 0.7 dynamic-slice_select_fusion.2
  536.4 167.0 %psum.31 = bf16[1,16,768]{2,1,0:T(8,128)(2,1)S(1)} all-reduce(bf16[1,16,768]{2,1,0:T(8,128)(2,1)S(1)} %dynamic-slice_select_fusion.2), channel_id=1, replica_groups=mesh['blk'=16,'neg'=32] {'neg'}, use_global_device_ids=true, to_apply=%region_2.2 | all-reduce | flops 12288 | bytes 49152 | tf_op jit(solution)/shard_map/while/body/eval_jaxpr/psum | solution.py:20
  703.4 0.0 copy-done.4
  703.4 0.1 compare_reduce_fusion
  703.5 0.1 copy.13
  703.6 0.1 broadcast_in_dim.46
  703.7 0.1 reshape.43
  703.8 0.0 collective-permute-done
  703.8 1.2 fusion.17
  705.1 0.0 copy-start.2
  705.1 0.6 copy-done.2
  705.7 0.1 select_reduce_fusion
  705.8 0.6 subtract_reduce_fusion
  706.5 0.2 fusion.4
  706.6 0.2 fusion
  706.8 0.0 copy-start.1
  706.8 0.7 copy.14
  707.5 0.0 all-reduce.3.cloned.1.call-update
  707.6 6.9 collective-permute-start.1
  714.5 1.0 fusion.1
  715.4 102.4 %psum.28 = f32[]{:T(128)} all-reduce(f32[]{:T(128)} %get-tuple-element.148), channel_id=1, replica_groups=mesh['blk'=16,'neg'=32] {'blk','neg'}, use_global_device_ids=true, to_apply=%region_8.9 | all-reduce | flops 1 | bytes 8 | tf_op jit(solution)/shard_map/psum | solution.py:63
  818.5 204.4 %all-reduce.3.cloned.1.call-done = bf16[4,16,768]{2,0,1:T(4,128)(2,1)} async-done(((bf16[4,16,768]{2,0,1:T(4,128)(2,1)}), bf16[4,16,768]{2,0,1:T(4,128)(2,1)}) %all-reduce.3.cloned.1.call-update) | async-done | bytes 98320 | tf_op jit(solution)/shard_map/psum | solution.py:75
  1022.8 1.2 fusion.11
  1024.1 0.1 copy.15
  1024.2 0.0 collective-permute-done.1
  1024.2 0.9 fusion.5
  (11 shorter events, 0.1 us)
Async XLA Ops:
  7.2 696.7 %copy-start = (bf16[128,768]{1,0:T(8,128)(2,1)S(1)}, bf16[128,768]{1,0:T(8,128)(2,1)}, u32[]{:S(2)}) copy-start(bf16[128,768]{1,0:T(8,128)(2,1)} %param.8) | copy-start | bytes 589828
  7.2 1015.7 %all-reduce.3.cloned.1.call-start = ((), (), s32[]{:S(2)}) async-start(), calls=%async_computation | async-start | bytes 196608 | tf_op jit(solution)/shard_map/psum | solution.py:75
  7.2 696.6 %collective-permute-start = (bf16[128,768]{1,0:T(8,128)(2,1)}, bf16[128,768]{1,0:T(8,128)(2,1)S(1)}, u32[]{:S(2)}, u32[]{:S(2)}) collective-permute-start(bf16[128,768]{1,0:T(8,128)(2,1)} %param.9), channel_id=1, source_target_pairs={{480,0},{0,32},{32,64},{64,96},{96,128},{128,160},{160,192},{192,2... | collective-permute-start | bytes 589832 | tf_op jit(solution)/shard_map/ppermute | solution.py:15
  11.4 0.7 copy-start.3
  11.4 0.7 copy-start.5
  12.1 691.3 %copy-start.4 = (s32[2,2]{1,0:T(2,128)S(1)}, s32[2,2]{1,0:T(2,128)}, u32[]{:S(2)}) copy-start(s32[2,2]{1,0:T(2,128)} %param.13) | copy-start | bytes 52
  705.1 0.7 copy-start.2
  706.8 7.6 copy-start.1
  707.6 316.6 %collective-permute-start.1 = (bf16[128,768]{1,0:T(8,128)(2,1)S(1)}, bf16[128,768]{1,0:T(8,128)(2,1)S(1)}, u32[]{:S(2)}, u32[]{:S(2)}) collective-permute-start(bf16[128,768]{1,0:T(8,128)(2,1)S(1)} %fusion), channel_id=1, source_target_pairs={{32,0},{64,32},{96,64},{128,96},{160,128},{192,160},{224,192},{256... | collective-permute-start | bytes 589832 | tf_op jit(solution)/shard_map/ppermute | solution.py:15
Sparse Core Ops, SparseCore 0:
  707.7 315.1 all-reduce.2
where the time goes:
time: 1030 us
  blocking collectives  776 us (75%)
  waiting for transfers between devices  204 us (20%)
  between operations  15.9 us (2%)
  starting transfers between devices  11.1 us (1%)
  loops' own time  10.4 us (1%)
    psum x4, blocking collectives, from_root(): return lax.psum(kept, axis)  673 us
    psum x1, waiting for transfers between devices, body(): lax.psum(hard_part.reshape(H, HB, width).astype(jnp.bfloat16), 'neg')  204 us
    psum x1, blocking collectives, body(): lax.psum(local_loss, ('blk', 'neg'))  102 us
  transfers between devices with their start and end apart: 3, of which 1 were waited for; matrix products, arithmetic and copies ran while one was open for 1% of the time, Pallas kernels for 0%

commit v1 on v0

v1 whole, which is shorter than its diff:
```python
import functools

import jax
import jax.numpy as jnp
from jax import lax
from jax.experimental import pallas as pl
from jax.experimental.pallas import tpu as pltpu
from jax.sharding import PartitionSpec as P

MESH = pl.DeviceIdType.MESH
H = 4
HB = 16
GQ = 64
NZ = 8
NX = 4
NYL = 4
ZORDER = (4, 3, 5, 2, 6, 1, 7)


def nt(a, b):
    return lax.dot_general(a, b, (((1,), (1,)), ((), ())), preferred_element_type=jnp.float32)


def nn(a, b):
    return lax.dot_general(a, b, (((1,), (0,)), ((), ())), preferred_element_type=jnp.float32)


def tn(a, b):
    return lax.dot_general(a, b, (((0,), (0,)), ((), ())), preferred_element_type=jnp.float32)


def kernel(
    n_all,
    q_hbm, p_hbm, pos_ref, own_ref, blk_ref, pick_ref,
    loss_ref, qg_ref, pg_ref,
    qv, pv, cv, hv, fsend, frecv, fx, fxr,
    gsend, grecv, gx, gxr, gt, cgs, cgr, og,
    l1, l1r, l2, l2r, l3, l3r,
    lsem, ss, fr_s, fx_s, fa_s, gr_s, gx_s, ga_s, c_s, l1_s, l2_s, l3_s,
):
    blk = lax.axis_index("blk")
    neg = lax.axis_index("neg")
    rows, width = p_hbm.shape
    scale = width ** (-0.5)
    half = width // 2
    z = neg // 4
    yh = (neg // 2) % 2
    core = neg % 2
    x = blk // NYL
    yl = blk % NYL
    y = yh * NYL + yl

    zpeer = {d: {"blk": blk, "neg": ((z + d) % NZ) * 4 + yh * 2 + core} for d in range(1, NZ)}
    ypeer = {
        d: {
            "blk": x * NYL + ((y + d) % 8) % NYL,
            "neg": z * 4 + (((y + d) % 8) // NYL) * 2 + core,
        }
        for d in range(1, 8)
    }
    xpeer = {}
    for d in range(1, 8):
        xpeer[d] = {
            "blk": ((x + d // 2) % NX) * NYL + yl,
            "neg": z * 4 + yh * 2 + (core + d % 2) % 2,
        }
    mpeer = {
        d: {"blk": blk, "neg": z * 4 + ((yh + d // 2) % 2) * 2 + (core + d % 2) % 2}
        for d in range(1, 4)
    }
    after = {"blk": (blk + 1) % 16, "neg": neg}
    before = {"blk": (blk + 15) % 16, "neg": neg}

    load_p = pltpu.make_async_copy(p_hbm, pv, lsem.at[0])
    load_q = pltpu.make_async_copy(q_hbm, qv, lsem.at[1])
    load_p.start()
    load_q.start()

    barrier = pltpu.get_barrier_semaphore()
    greet = list(zpeer.values()) + list(ypeer.values()) + list(xpeer.values())
    greet += [mpeer[3], after, before]
    for who in greet:
        pl.semaphore_signal(barrier, inc=1, device_id=who, device_id_type=MESH)

    srow = lax.broadcasted_iota(jnp.int32, (H * HB, rows), 0)
    owner = jnp.zeros_like(srow)
    place = jnp.zeros_like(srow)
    for h in range(H):
        owner = jnp.where(srow // HB == h, own_ref[:, h:h + 1], owner)
        place = jnp.where(srow // HB == h, blk_ref[:, h:h + 1], place)
    chosen = (owner == neg) & (place * HB + srow % HB == lax.broadcasted_iota(jnp.int32, srow.shape, 1))
    sel = chosen.astype(jnp.float32).astype(jnp.bfloat16)
    load_p.wait()
    fsend[...] = nn(sel, pv[...]).astype(jnp.bfloat16)
    pl.semaphore_wait(barrier, len(greet))

    sent = []

    def push(src, dst, send, recv, who):
        copy = pltpu.make_async_remote_copy(
            src_ref=src, dst_ref=dst, send_sem=send, recv_sem=recv,
            device_id=who, device_id_type=MESH,
        )
        copy.start()
        sent.append(copy)
        return copy

    def part(ref, index):
        return ref.at[
            pl.ds(pl.multiple_of((index // 2) * HB, HB), HB),
            pl.ds(pl.multiple_of((index % 2) * half, half), half),
        ]

    sends = iter(range(64))

    def scatter(buf, land, sem):
        return [
            push(part(buf, (z + d) % NZ), land.at[d - 1], ss.at[next(sends)], sem.at[d - 1], zpeer[d])
            for d in ZORDER
        ]

    def gather(buf, sem):
        return [
            push(part(buf, z), part(buf, z), ss.at[next(sends)], sem.at[d - 1], zpeer[d])
            for d in ZORDER
        ]

    def middle(buf, land, sem):
        return [
            push(buf, land.at[d - 1], ss.at[next(sends)], sem.at[d - 1], mpeer[d]) for d in (3, 2, 1)
        ]

    def arrive(copies):
        for copy in copies:
            copy.wait_recv()

    def load_part(ref):
        return part(ref, z)[...].astype(jnp.float32)

    f1 = scatter(fsend, frecv, fr_s)
    cyc = push(pv, cv, ss.at[next(sends)], c_s.at[0], after)

    load_q.wait()
    q = qv[...]
    s0 = nt(pv[...], q) * scale

    arrive(f1)
    fx[...] = (load_part(fsend) + jnp.sum(frecv[...].astype(jnp.float32), axis=0)).astype(jnp.bfloat16)
    f2 = middle(fx, fxr, fx_s)
    arrive(f2)
    part(hv, z)[...] = (
        fx[...].astype(jnp.float32) + jnp.sum(fxr[...].astype(jnp.float32), axis=0)
    ).astype(jnp.bfloat16)
    f3 = gather(hv, fa_s)
    cyc.wait_recv()
    s1 = nt(cv[...], q) * scale
    arrive(f3)
    s2 = nt(hv[...], q) * scale

    lane = lax.broadcasted_iota(jnp.int32, s2.shape, 1)
    slot = lax.broadcasted_iota(jnp.int32, s2.shape, 0) // HB
    first = jnp.where(lane < GQ, pick_ref[0:1, 0:1], pick_ref[1:2, 0:1])
    second = jnp.where(lane < GQ, pick_ref[0:1, 1:2], pick_ref[1:2, 1:2])
    s2 = jnp.where((slot == first) | (slot == second), s2, -jnp.inf)
    top = jnp.maximum(
        jnp.maximum(jnp.max(s0, axis=0, keepdims=True), jnp.max(s1, axis=0, keepdims=True)),
        jnp.max(s2, axis=0, keepdims=True),
    )
    total = (
        jnp.sum(jnp.exp(s0 - top), axis=0, keepdims=True)
        + jnp.sum(jnp.exp(s1 - top), axis=0, keepdims=True)
        + jnp.sum(jnp.exp(s2 - top), axis=0, keepdims=True)
    )
    lse = top + jnp.log(total)
    hot = lax.broadcasted_iota(jnp.int32, s0.shape, 0) == pos_ref[...]

    g2 = jnp.exp(s2 - lse).astype(jnp.bfloat16)
    gsend[...] = (nn(g2, q) * scale).astype(jnp.bfloat16)
    b1 = scatter(gsend, grecv, gr_s)

    l1[...] = lse - jnp.sum(jnp.where(hot, s0, 0.0), axis=0, keepdims=True)
    a1 = [push(l1, l1r.at[d - 1], ss.at[next(sends)], l1_s.at[d - 1], zpeer[d]) for d in ZORDER]

    g1 = jnp.exp(s1 - lse).astype(jnp.bfloat16)
    cgs[...] = (nn(g1, q) * scale).astype(jnp.bfloat16)
    back = push(cgs, cgr, ss.at[next(sends)], c_s.at[1], before)

    g0 = (jnp.exp(s0 - lse) - hot.astype(jnp.float32)).astype(jnp.bfloat16)
    og[...] = nn(g0, q) * scale
    qg_ref[...] = ((tn(g0, pv[...]) + tn(g1, cv[...]) + tn(g2, hv[...])) * scale).astype(jnp.bfloat16)

    arrive(b1)
    gx[...] = (load_part(gsend) + jnp.sum(grecv[...].astype(jnp.float32), axis=0)).astype(jnp.bfloat16)
    b2 = middle(gx, gxr, gx_s)
    arrive(a1)
    l2[...] = l1[...] + jnp.sum(l1r[...], axis=0)
    a2 = [push(l2, l2r.at[d - 1], ss.at[next(sends)], l2_s.at[d - 1], ypeer[d]) for d in ZORDER]
    arrive(b2)
    part(gt, z)[...] = (
        gx[...].astype(jnp.float32) + jnp.sum(gxr[...].astype(jnp.float32), axis=0)
    ).astype(jnp.bfloat16)
    b3 = gather(gt, ga_s)
    arrive(a2)
    l3[...] = l2[...] + jnp.sum(l2r[...], axis=0)
    a3 = [push(l3, l3r.at[d - 1], ss.at[next(sends)], l3_s.at[d - 1], xpeer[d]) for d in range(1, 8)]
    back.wait_recv()
    og[...] += cgr[...].astype(jnp.float32)
    arrive(a3)
    loss_ref[0, 0] = jnp.sum(l3[...] + jnp.sum(l3r[...], axis=0)) / n_all
    arrive(b3)
    pg_ref[...] = (og[...] + tn(sel, gt[...])).astype(jnp.bfloat16)
    for copy in sent:
        copy.wait_send()


def body(queries, passages, positive, hard_owner, hard_block, hard_pick):
    rows, width = passages.shape
    n_all = rows * lax.axis_size("blk") * lax.axis_size("neg")
    bf = jnp.bfloat16
    f32 = jnp.float32
    any_space = pl.BlockSpec(memory_space=pl.ANY)
    vmem = pl.BlockSpec(memory_space=pltpu.VMEM)
    smem = pl.BlockSpec(memory_space=pltpu.SMEM)
    half = width // 2
    dma = pltpu.SemaphoreType.DMA
    loss, query_grad, passage_grad = pl.pallas_call(
        functools.partial(kernel, n_all),
        out_shape=(
            jax.ShapeDtypeStruct((1, 1), f32),
            jax.ShapeDtypeStruct((rows, width), bf),
            jax.ShapeDtypeStruct((rows, width), bf),
        ),
        in_specs=[any_space, any_space, vmem, vmem, vmem, vmem],
        out_specs=(smem, vmem, vmem),
        scratch_shapes=[
            pltpu.VMEM((rows, width), bf),
            pltpu.VMEM((rows, width), bf),
            pltpu.VMEM((rows, width), bf),
            pltpu.VMEM((H * HB, width), bf),
            pltpu.VMEM((H * HB, width), bf),
            pltpu.VMEM((NZ - 1, HB, half), bf),
            pltpu.VMEM((HB, half), bf),
            pltpu.VMEM((3, HB, half), bf),
            pltpu.VMEM((H * HB, width), bf),
            pltpu.VMEM((NZ - 1, HB, half), bf),
            pltpu.VMEM((HB, half), bf),
            pltpu.VMEM((3, HB, half), bf),
            pltpu.VMEM((H * HB, width), bf),
            pltpu.VMEM((rows, width), bf),
            pltpu.VMEM((rows, width), bf),
            pltpu.VMEM((rows, width), f32),
            pltpu.VMEM((1, rows), f32),
            pltpu.VMEM((7, 1, rows), f32),
            pltpu.VMEM((1, rows), f32),
            pltpu.VMEM((7, 1, rows), f32),
            pltpu.VMEM((1, rows), f32),
            pltpu.VMEM((7, 1, rows), f32),
            dma((2,)),
            dma((64,)),
            dma((NZ - 1,)),
            dma((3,)),
            dma((NZ - 1,)),
            dma((NZ - 1,)),
            dma((3,)),
            dma((NZ - 1,)),
            dma((2,)),
            dma((7,)),
            dma((7,)),
            dma((7,)),
        ],
        compiler_params=pltpu.CompilerParams(collective_id=0, has_side_effects=True),
        name="retriever",
    )(queries, passages, positive.reshape(1, rows), hard_owner, hard_block, hard_pick)
    return (loss[0, 0], query_grad, passage_grad)


def solution(mesh):
    placed = (
        P(("blk", "neg"), None),
        P(("blk", "neg"), None),
        P(("blk", "neg")),
        P("blk", None),
        P("blk", None),
        P(("blk", "neg"), None),
    )
    return jax.shard_map(
        body,
        mesh=mesh,
        in_specs=placed,
        out_specs=(P(), P(("blk", "neg"), None), P(("blk", "neg"), None)),
        check_vma=False,
    )
```

time: 1030 us -> 52.5 us (0.05)
  blocking collectives: 776 us -> 0 us
  waiting for transfers between devices: 204 us -> 0 us
  Pallas kernels: 0 us -> 47.5 us
  between operations: 15.9 us -> 2.47 us
  starting transfers between devices: 11.1 us -> 0 us
  loops' own time: 10.4 us -> 0 us
    psum x5 -> x0, blocking collectives: 776 us -> none  [the longest x4 673 us: from_root(): return lax.psum(kept, axis)]
    psum x1 -> x0, waiting for transfers between devices: 204 us -> none  [body(): lax.psum(hard_part.reshape(H, HB, width).astype(jnp.bfloat16), 'neg')]
    pallas_call x0 -> x1, Pallas kernels: none -> 47.5 us  [body(): pl.pallas_call(functools.partial(kernel, n_all), out_shape=(jax.ShapeDtyp...]
    ppermute x2 -> x0, starting transfers between devices: 11.1 us -> none  [from_behind(): return lax.ppermute(block, axis, route)]
    another operation x1 -> x0, loops' own time: 10.4 us -> none  [body(): hard = lax.fori_loop(0, H, fetch, jnp.zeros((H, HB, width), jnp.bfloat16))]
  transfers between devices with their start and end apart: 3 -> 0, of which waited for: 1 -> 0; matrix products, arithmetic and copies ran while one was open for 1% -> 0% of each run, Pallas kernels for 0% -> 0%
where the time goes in v1:
time: 52.5 us; the launch traced here: 52.3 us
  Pallas kernels  47.5 us (90%)
  between operations  2.47 us (5%)
  local copies, waits for them, and re-layouts  2.34 us (4%)
    pallas_call x1, Pallas kernels, body(): pl.pallas_call(functools.partial(kernel, n_all), out_shape=(jax.ShapeDtyp...  47.5 us
    unnamed x4, local copies, waits for them, and re-layouts  2.34 us

profile of v1, /device:TPU:1, one launch (start us, length us, event | category | flops | bytes accessed | tf_op | source)
XLA Modules:
  0.0 52.3 jit_solution(17730836024623506732)
XLA Ops:
  0.6 47.5 %retriever.1 = (f32[1,1]{1,0:T(1,128)}, bf16[128,768]{1,0:T(8,128)(2,1)}, bf16[128,768]{1,0:T(8,128)(2,1)}) custom-call(bf16[128,768]{1,0:T(8,128)(2,1)} %q_hbm.1, bf16[128,768]{1,0:T(8,128)(2,1)} %p_hbm.1, s32[1,128]{1,0:T(1,128)} %bitcast.2, s32[1,4]{1,0:T(1,128)} %own_ref.1, s32[1,4]{1,0:T(1,128)} %blk_ref.1, s32[2,2]{1,0:T(2,128)} %pick_ref.1), custom_call_target="tpu_custom_call" | custom-call | tf_op jit(solution)/shard_map/retriever/pallas_call | solution.py:226
  48.8 0.0 copy-start
  48.8 1.7 %copy.13 = bf16[128,768]{1,0:T(8,128)(2,1)} copy(bf16[128,768]{1,0:T(8,128)(2,1)} %get-tuple-element.13) | data formatting | bytes 393216
  50.5 0.0 copy-done
  50.5 0.7 %copy.14 = bf16[128,768]{1,0:T(8,128)(2,1)} copy(bf16[128,768]{1,0:T(8,128)(2,1)S(1)} %copy-done) | data formatting | bytes 393216
Async XLA Ops:
  48.8 1.7 %copy-start = (bf16[128,768]{1,0:T(8,128)(2,1)S(1)}, bf16[128,768]{1,0:T(8,128)(2,1)}, u32[]{:S(2)}) copy-start(bf16[128,768]{1,0:T(8,128)(2,1)} %get-tuple-element.14) | copy-start | bytes 589828

commit v2 on v1

--- a/solution.py
+++ b/solution.py
@@ -31,8 +31,9 @@
 
 def kernel(
     n_all,
-    q_hbm, p_hbm, pos_ref, own_ref, blk_ref, pick_ref,
-    loss_ref, qg_ref, pg_ref,
+    q_hbm, p_hbm, pos_hbm, own_hbm, blk_hbm, pick_hbm,
+    loss_ref, out_ref,
+    pos_ref, own_ref, blk_ref, pick_ref,
     qv, pv, cv, hv, fsend, frecv, fx, fxr,
     gsend, grecv, gx, gxr, gt, cgs, cgr, og,
     l1, l1r, l2, l2r, l3, l3r,
@@ -73,8 +74,16 @@
 
     load_p = pltpu.make_async_copy(p_hbm, pv, lsem.at[0])
     load_q = pltpu.make_async_copy(q_hbm, qv, lsem.at[1])
+    load_own = pltpu.make_async_copy(own_hbm, own_ref, lsem.at[2])
+    load_blk = pltpu.make_async_copy(blk_hbm, blk_ref, lsem.at[3])
+    load_pos = pltpu.make_async_copy(pos_hbm, pos_ref, lsem.at[4])
+    load_pick = pltpu.make_async_copy(pick_hbm, pick_ref, lsem.at[5])
     load_p.start()
+    load_own.start()
+    load_blk.start()
     load_q.start()
+    load_pos.start()
+    load_pick.start()
 
     barrier = pltpu.get_barrier_semaphore()
     greet = list(zpeer.values()) + list(ypeer.values()) + list(xpeer.values())
@@ -82,6 +91,8 @@
     for who in greet:
         pl.semaphore_signal(barrier, inc=1, device_id=who, device_id_type=MESH)
 
+    load_own.wait()
+    load_blk.wait()
     srow = lax.broadcasted_iota(jnp.int32, (H * HB, rows), 0)
     owner = jnp.zeros_like(srow)
     place = jnp.zeros_like(srow)
@@ -141,6 +152,8 @@
     cyc = push(pv, cv, ss.at[next(sends)], c_s.at[0], after)
 
     load_q.wait()
+    load_pos.wait()
+    load_pick.wait()
     q = qv[...]
     s0 = nt(pv[...], q) * scale
 
@@ -187,7 +200,7 @@
 
     g0 = (jnp.exp(s0 - lse) - hot.astype(jnp.float32)).astype(jnp.bfloat16)
     og[...] = nn(g0, q) * scale
-    qg_ref[...] = ((tn(g0, pv[...]) + tn(g1, cv[...]) + tn(g2, hv[...])) * scale).astype(jnp.bfloat16)
+    out_ref[0] = ((tn(g0, pv[...]) + tn(g1, cv[...]) + tn(g2, hv[...])) * scale).astype(jnp.bfloat16)
 
     arrive(b1)
     gx[...] = (load_part(gsend) + jnp.sum(grecv[...].astype(jnp.float32), axis=0)).astype(jnp.bfloat16)
@@ -208,7 +221,7 @@
     arrive(a3)
     loss_ref[0, 0] = jnp.sum(l3[...] + jnp.sum(l3r[...], axis=0)) / n_all
     arrive(b3)
-    pg_ref[...] = (og[...] + tn(sel, gt[...])).astype(jnp.bfloat16)
+    out_ref[1] = (og[...] + tn(sel, gt[...])).astype(jnp.bfloat16)
     for copy in sent:
         copy.wait_send()
 
@@ -223,16 +236,19 @@
     smem = pl.BlockSpec(memory_space=pltpu.SMEM)
     half = width // 2
     dma = pltpu.SemaphoreType.DMA
-    loss, query_grad, passage_grad = pl.pallas_call(
+    loss, grads = pl.pallas_call(
         functools.partial(kernel, n_all),
         out_shape=(
             jax.ShapeDtypeStruct((1, 1), f32),
-            jax.ShapeDtypeStruct((rows, width), bf),
-            jax.ShapeDtypeStruct((rows, width), bf),
+            pltpu.VMEM((2, rows, width), bf),
         ),
-        in_specs=[any_space, any_space, vmem, vmem, vmem, vmem],
-        out_specs=(smem, vmem, vmem),
+        in_specs=[any_space] * 6,
+        out_specs=(smem, vmem),
         scratch_shapes=[
+            pltpu.VMEM((1, rows), jnp.int32),
+            pltpu.VMEM(hard_owner.shape, jnp.int32),
+            pltpu.VMEM(hard_block.shape, jnp.int32),
+            pltpu.VMEM(hard_pick.shape, jnp.int32),
             pltpu.VMEM((rows, width), bf),
             pltpu.VMEM((rows, width), bf),
             pltpu.VMEM((rows, width), bf),
@@ -255,7 +271,7 @@
             pltpu.VMEM((7, 1, rows), f32),
             pltpu.VMEM((1, rows), f32),
             pltpu.VMEM((7, 1, rows), f32),
-            dma((2,)),
+            dma((6,)),
             dma((64,)),
             dma((NZ - 1,)),
             dma((3,)),
@@ -271,7 +287,7 @@
         compiler_params=pltpu.CompilerParams(collective_id=0, has_side_effects=True),
         name="retriever",
     )(queries, passages, positive.reshape(1, rows), hard_owner, hard_block, hard_pick)
-    return (loss[0, 0], query_grad, passage_grad)
+    return (loss[0, 0], grads[0], grads[1])
 
 
 def solution(mesh):

time: 52.5 us -> 50.1 us (0.954)
  local copies, waits for them, and re-layouts: 2.34 us -> 0.77 us
  Pallas kernels: 47.5 us -> 46.7 us
    unnamed x4 -> x0, local copies, waits for them, and re-layouts: 2.34 us -> none
    pallas_call x1, Pallas kernels: 47.5 us -> 46.7 us  [body(): pl.pallas_call(functools.partial(kernel, n_all), out_shape=(jax.ShapeDtyp...]
    squeeze x0 -> x1, local copies, waits for them, and re-layouts: none -> 0.77 us  [body(): return (loss[0, 0], grads[0], grads[1])]
where the time goes in v2:
time: 50.1 us; the launch traced here: 49.9 us
  Pallas kernels  46.7 us (93%)
  between operations  2.4 us (5%)
  local copies, waits for them, and re-layouts  0.77 us (2%)
    pallas_call x1, Pallas kernels, body(): pl.pallas_call(functools.partial(kernel, n_all), out_shape=(jax.ShapeDtyp...  46.7 us

profile of v2, /device:TPU:1, one launch (start us, length us, event | category | flops | bytes accessed | tf_op | source)
XLA Modules:
  0.0 49.9 jit_solution(9017239163056747863)
XLA Ops:
  0.6 46.7 %retriever.1 = (f32[1,1]{1,0:T(1,128)}, bf16[2,128,768]{2,1,0:T(8,128)(2,1)S(1)}) custom-call(bf16[128,768]{1,0:T(8,128)(2,1)} %q_hbm.1, bf16[128,768]{1,0:T(8,128)(2,1)} %p_hbm.1, s32[1,128]{1,0:T(1,128)} %bitcast.6, s32[1,4]{1,0:T(1,128)} %own_hbm.1, s32[1,4]{1,0:T(1,128)} %blk_hbm.1, s32[2,2]{1,0:T(2,128)} %pick_hbm.1), custom_call_target="tpu_custom_call" | custom-call | tf_op jit(solution)/shard_map/retriever/pallas_call | solution.py:239
  47.4 0.8 %slice_bitcast_fusion = (bf16[128,768]{1,0:T(8,128)(2,1)}, bf16[128,768]{1,0:T(8,128)(2,1)}) fusion(bf16[2,128,768]{2,1,0:T(8,128)(2,1)S(1)} %get-tuple-element.6), kind=kLoop, calls=%fused_computation | loop fusion | bytes 786432 | tf_op jit(solution)/shard_map/squeeze | solution.py:290

commit v3 on v2

--- a/solution.py
+++ b/solution.py
@@ -116,6 +116,11 @@
         sent.append(copy)
         return copy
 
+    def leave():
+        for copy in sent:
+            copy.wait_send()
+        sent.clear()
+
     def part(ref, index):
         return ref.at[
             pl.ds(pl.multiple_of((index // 2) * HB, HB), HB),
@@ -151,11 +156,23 @@
     f1 = scatter(fsend, frecv, fr_s)
     cyc = push(pv, cv, ss.at[next(sends)], c_s.at[0], after)
 
+    scol = lax.broadcasted_iota(jnp.int32, (rows, H * HB), 1)
+    owner_t = jnp.zeros_like(scol)
+    place_t = jnp.zeros_like(scol)
+    for h in range(H):
+        owner_t = jnp.where(scol // HB == h, own_ref[:, h:h + 1], owner_t)
+        place_t = jnp.where(scol // HB == h, blk_ref[:, h:h + 1], place_t)
+    chosen_t = (owner_t == neg) & (
+        place_t * HB + scol % HB == lax.broadcasted_iota(jnp.int32, scol.shape, 0)
+    )
+    sel_t = chosen_t.astype(jnp.float32).astype(jnp.bfloat16)
     load_q.wait()
     load_pos.wait()
     load_pick.wait()
     q = qv[...]
     s0 = nt(pv[...], q) * scale
+    hot = lax.broadcasted_iota(jnp.int32, s0.shape, 0) == pos_ref[...]
+    spos = jnp.sum(jnp.where(hot, s0, 0.0), axis=0, keepdims=True)
 
     arrive(f1)
     fx[...] = (load_part(fsend) + jnp.sum(frecv[...].astype(jnp.float32), axis=0)).astype(jnp.bfloat16)
@@ -167,31 +184,28 @@
     f3 = gather(hv, fa_s)
     cyc.wait_recv()
     s1 = nt(cv[...], q) * scale
+    top01 = jnp.maximum(jnp.max(s0, axis=0, keepdims=True), jnp.max(s1, axis=0, keepdims=True))
+    sum01 = jnp.sum(jnp.exp(s0 - top01), axis=0, keepdims=True) + jnp.sum(
+        jnp.exp(s1 - top01), axis=0, keepdims=True
+    )
+    lane = lax.broadcasted_iota(jnp.int32, (H * HB, rows), 1)
+    slot = lax.broadcasted_iota(jnp.int32, (H * HB, rows), 0) // HB
+    first = jnp.where(lane < GQ, pick_ref[0:1, 0:1], pick_ref[1:2, 0:1])
+    second = jnp.where(lane < GQ, pick_ref[0:1, 1:2], pick_ref[1:2, 1:2])
+    picked = (slot == first) | (slot == second)
     arrive(f3)
     s2 = nt(hv[...], q) * scale
 
-    lane = lax.broadcasted_iota(jnp.int32, s2.shape, 1)
-    slot = lax.broadcasted_iota(jnp.int32, s2.shape, 0) // HB
-    first = jnp.where(lane < GQ, pick_ref[0:1, 0:1], pick_ref[1:2, 0:1])
-    second = jnp.where(lane < GQ, pick_ref[0:1, 1:2], pick_ref[1:2, 1:2])
-    s2 = jnp.where((slot == first) | (slot == second), s2, -jnp.inf)
-    top = jnp.maximum(
-        jnp.maximum(jnp.max(s0, axis=0, keepdims=True), jnp.max(s1, axis=0, keepdims=True)),
-        jnp.max(s2, axis=0, keepdims=True),
-    )
-    total = (
-        jnp.sum(jnp.exp(s0 - top), axis=0, keepdims=True)
-        + jnp.sum(jnp.exp(s1 - top), axis=0, keepdims=True)
-        + jnp.sum(jnp.exp(s2 - top), axis=0, keepdims=True)
-    )
+    s2 = jnp.where(picked, s2, -jnp.inf)
+    top = jnp.maximum(top01, jnp.max(s2, axis=0, keepdims=True))
+    total = sum01 * jnp.exp(top01 - top) + jnp.sum(jnp.exp(s2 - top), axis=0, keepdims=True)
     lse = top + jnp.log(total)
-    hot = lax.broadcasted_iota(jnp.int32, s0.shape, 0) == pos_ref[...]
 
     g2 = jnp.exp(s2 - lse).astype(jnp.bfloat16)
     gsend[...] = (nn(g2, q) * scale).astype(jnp.bfloat16)
     b1 = scatter(gsend, grecv, gr_s)
 
-    l1[...] = lse - jnp.sum(jnp.where(hot, s0, 0.0), axis=0, keepdims=True)
+    l1[...] = lse - spos
     a1 = [push(l1, l1r.at[d - 1], ss.at[next(sends)], l1_s.at[d - 1], zpeer[d]) for d in ZORDER]
 
     g1 = jnp.exp(s1 - lse).astype(jnp.bfloat16)
@@ -202,6 +216,7 @@
     og[...] = nn(g0, q) * scale
     out_ref[0] = ((tn(g0, pv[...]) + tn(g1, cv[...]) + tn(g2, hv[...])) * scale).astype(jnp.bfloat16)
 
+    leave()
     arrive(b1)
     gx[...] = (load_part(gsend) + jnp.sum(grecv[...].astype(jnp.float32), axis=0)).astype(jnp.bfloat16)
     b2 = middle(gx, gxr, gx_s)
@@ -220,10 +235,9 @@
     og[...] += cgr[...].astype(jnp.float32)
     arrive(a3)
     loss_ref[0, 0] = jnp.sum(l3[...] + jnp.sum(l3r[...], axis=0)) / n_all
+    leave()
     arrive(b3)
-    out_ref[1] = (og[...] + tn(sel, gt[...])).astype(jnp.bfloat16)
-    for copy in sent:
-        copy.wait_send()
+    out_ref[1] = (og[...] + nn(sel_t, gt[...])).astype(jnp.bfloat16)
 
 
 def body(queries, passages, positive, hard_owner, hard_block, hard_pick):
@@ -239,7 +253,7 @@
     loss, grads = pl.pallas_call(
         functools.partial(kernel, n_all),
         out_shape=(
-            jax.ShapeDtypeStruct((1, 1), f32),
+            pltpu.SMEM((1, 1), f32),
             pltpu.VMEM((2, rows, width), bf),
         ),
         in_specs=[any_space] * 6,

time: 50.1 us -> 48.2 us (0.962)
  between operations: 2.4 us -> 1.16 us
  Pallas kernels: 46.7 us -> 46.1 us
    pallas_call x1, Pallas kernels: 46.7 us -> 46.1 us  [body(): pl.pallas_call(functools.partial(kernel, n_all), out_shape=(pltpu.SMEM((1...]
where the time goes in v3:
time: 48.2 us; the launch traced here: 48 us
  Pallas kernels  46.1 us (96%)
  between operations  1.16 us (2%)
  local copies, waits for them, and re-layouts  0.77 us (2%)
    pallas_call x1, Pallas kernels, body(): pl.pallas_call(functools.partial(kernel, n_all), out_shape=(pltpu.SMEM((1...  46.1 us

profile of v3, /device:TPU:1, one launch (start us, length us, event | category | flops | bytes accessed | tf_op | source)
XLA Modules:
  0.0 48.0 jit_solution(6412031056411447268)
XLA Ops:
  0.6 46.1 %retriever.1 = (f32[1,1]{1,0:T(1,128)S(4)}, bf16[2,128,768]{2,1,0:T(8,128)(2,1)S(1)}) custom-call(bf16[128,768]{1,0:T(8,128)(2,1)} %q_hbm.1, bf16[128,768]{1,0:T(8,128)(2,1)} %p_hbm.1, s32[1,128]{1,0:T(1,128)} %bitcast.6, s32[1,4]{1,0:T(1,128)} %own_hbm.1, s32[1,4]{1,0:T(1,128)} %blk_hbm.1, s32[2,2]{1,0:T(2,128)} %pick_hbm.1), custom_call_target="tpu_custom_call" | custom-call | tf_op jit(solution)/shard_map/retriever/pallas_call | solution.py:253
  47.3 0.8 %slice_bitcast_fusion = (bf16[128,768]{1,0:T(8,128)(2,1)}, bf16[128,768]{1,0:T(8,128)(2,1)}) fusion(bf16[2,128,768]{2,1,0:T(8,128)(2,1)S(1)} %get-tuple-element.6), kind=kLoop, calls=%fused_computation | loop fusion | bytes 786432 | tf_op jit(solution)/shard_map/squeeze | solution.py:304

commit v4 on v3

--- a/solution.py
+++ b/solution.py
@@ -79,17 +79,19 @@
     load_pos = pltpu.make_async_copy(pos_hbm, pos_ref, lsem.at[4])
     load_pick = pltpu.make_async_copy(pick_hbm, pick_ref, lsem.at[5])
     load_p.start()
+
+    barrier = pltpu.get_barrier_semaphore()
+    greet = [zpeer[4], mpeer[3], ypeer[4], after, before]
+    greet += [zpeer[d] for d in ZORDER[1:]]
+    greet += [ypeer[d] for d in ZORDER[1:]]
+    greet += [xpeer[d] for d in (5, 4, 3, 2, 7, 6, 1)]
+    for who in greet:
+        pl.semaphore_signal(barrier, inc=1, device_id=who, device_id_type=MESH)
     load_own.start()
     load_blk.start()
     load_q.start()
     load_pos.start()
     load_pick.start()
-
-    barrier = pltpu.get_barrier_semaphore()
-    greet = list(zpeer.values()) + list(ypeer.values()) + list(xpeer.values())
-    greet += [mpeer[3], after, before]
-    for who in greet:
-        pl.semaphore_signal(barrier, inc=1, device_id=who, device_id_type=MESH)
 
     load_own.wait()
     load_blk.wait()
@@ -201,6 +203,8 @@
     total = sum01 * jnp.exp(top01 - top) + jnp.sum(jnp.exp(s2 - top), axis=0, keepdims=True)
     lse = top + jnp.log(total)
 
+    forward = list(sent)
+    sent.clear()
     g2 = jnp.exp(s2 - lse).astype(jnp.bfloat16)
     gsend[...] = (nn(g2, q) * scale).astype(jnp.bfloat16)
     b1 = scatter(gsend, grecv, gr_s)
@@ -216,7 +220,8 @@
     og[...] = nn(g0, q) * scale
     out_ref[0] = ((tn(g0, pv[...]) + tn(g1, cv[...]) + tn(g2, hv[...])) * scale).astype(jnp.bfloat16)
 
-    leave()
+    for copy in forward:
+        copy.wait_send()
     arrive(b1)
     gx[...] = (load_part(gsend) + jnp.sum(grecv[...].astype(jnp.float32), axis=0)).astype(jnp.bfloat16)
     b2 = middle(gx, gxr, gx_s)

time: 48.2 us -> 47.6 us (0.988)
  Pallas kernels: 46.1 us -> 45.5 us
    pallas_call x1, Pallas kernels: 46.1 us -> 45.5 us  [body(): pl.pallas_call(functools.partial(kernel, n_all), out_shape=(pltpu.SMEM((1...]
where the time goes in v4:
time: 47.6 us; the launch traced here: 47.5 us
  Pallas kernels  45.5 us (96%)
  between operations  1.16 us (2%)
  local copies, waits for them, and re-layouts  0.77 us (2%)
    pallas_call x1, Pallas kernels, body(): pl.pallas_call(functools.partial(kernel, n_all), out_shape=(pltpu.SMEM((1...  45.5 us

profile of v4, /device:TPU:1, one launch (start us, length us, event | category | flops | bytes accessed | tf_op | source)
XLA Modules:
  0.0 47.5 jit_solution(2772745781563875286)
XLA Ops:
  0.6 45.5 %retriever.1 = (f32[1,1]{1,0:T(1,128)S(4)}, bf16[2,128,768]{2,1,0:T(8,128)(2,1)S(1)}) custom-call(bf16[128,768]{1,0:T(8,128)(2,1)} %q_hbm.1, bf16[128,768]{1,0:T(8,128)(2,1)} %p_hbm.1, s32[1,128]{1,0:T(1,128)} %bitcast.6, s32[1,4]{1,0:T(1,128)} %own_hbm.1, s32[1,4]{1,0:T(1,128)} %blk_hbm.1, s32[2,2]{1,0:T(2,128)} %pick_hbm.1), custom_call_target="tpu_custom_call" | custom-call | tf_op jit(solution)/shard_map/retriever/pallas_call | solution.py:258
  46.7 0.8 %slice_bitcast_fusion = (bf16[128,768]{1,0:T(8,128)(2,1)}, bf16[128,768]{1,0:T(8,128)(2,1)}) fusion(bf16[2,128,768]{2,1,0:T(8,128)(2,1)S(1)} %get-tuple-element.6), kind=kLoop, calls=%fused_computation | loop fusion | bytes 786432 | tf_op jit(solution)/shard_map/squeeze | solution.py:309

commit v5 on v4

--- a/solution.py
+++ b/solution.py
@@ -37,7 +37,7 @@
     qv, pv, cv, hv, fsend, frecv, fx, fxr,
     gsend, grecv, gx, gxr, gt, cgs, cgr, og,
     l1, l1r, l2, l2r, l3, l3r,
-    lsem, ss, fr_s, fx_s, fa_s, gr_s, gx_s, ga_s, c_s, l1_s, l2_s, l3_s,
+    lsem, fr_s, fx_s, fa_s, gr_s, gx_s, ga_s, c_s, k_s, l1_s, l2_s, l3_s,
 ):
     blk = lax.axis_index("blk")
     neg = lax.axis_index("neg")
@@ -107,21 +107,23 @@
     fsend[...] = nn(sel, pv[...]).astype(jnp.bfloat16)
     pl.semaphore_wait(barrier, len(greet))
 
-    sent = []
-
-    def push(src, dst, send, recv, who):
-        copy = pltpu.make_async_remote_copy(
-            src_ref=src, dst_ref=dst, send_sem=send, recv_sem=recv,
+    def push(src, dst, sems, who):
+        pltpu.make_async_remote_copy(
+            src_ref=src, dst_ref=dst, send_sem=sems.at[0], recv_sem=sems.at[1],
             device_id=who, device_id_type=MESH,
+        ).start()
+
+    def all_of(ref, sems):
+        return pltpu.make_async_remote_copy(
+            src_ref=ref, dst_ref=ref, send_sem=sems.at[0], recv_sem=sems.at[1],
+            device_id=after, device_id_type=MESH,
         )
-        copy.start()
-        sent.append(copy)
-        return copy
-
-    def leave():
-        for copy in sent:
-            copy.wait_send()
-        sent.clear()
+
+    def arrive(ref, sems):
+        all_of(ref, sems).wait_recv()
+
+    def leave(ref, sems):
+        all_of(ref, sems).wait_send()
 
     def part(ref, index):
         return ref.at[
@@ -129,34 +131,23 @@
             pl.ds(pl.multiple_of((index % 2) * half, half), half),
         ]
 
-    sends = iter(range(64))
-
-    def scatter(buf, land, sem):
-        return [
-            push(part(buf, (z + d) % NZ), land.at[d - 1], ss.at[next(sends)], sem.at[d - 1], zpeer[d])
-            for d in ZORDER
-        ]
-
-    def gather(buf, sem):
-        return [
-            push(part(buf, z), part(buf, z), ss.at[next(sends)], sem.at[d - 1], zpeer[d])
-            for d in ZORDER
-        ]
-
-    def middle(buf, land, sem):
-        return [
-            push(buf, land.at[d - 1], ss.at[next(sends)], sem.at[d - 1], mpeer[d]) for d in (3, 2, 1)
-        ]
-
-    def arrive(copies):
-        for copy in copies:
-            copy.wait_recv()
+    def scatter(buf, land, sems):
+        for d in ZORDER:
+            push(part(buf, (z + d) % NZ), land.at[d - 1], sems, zpeer[d])
+
+    def gather(buf, sems):
+        for d in ZORDER:
+            push(part(buf, z), part(buf, z), sems, zpeer[d])
+
+    def middle(buf, land, sems):
+        for d in (3, 2, 1):
+            push(buf, land.at[d - 1], sems, mpeer[d])
 
     def load_part(ref):
         return part(ref, z)[...].astype(jnp.float32)
 
-    f1 = scatter(fsend, frecv, fr_s)
-    cyc = push(pv, cv, ss.at[next(sends)], c_s.at[0], after)
+    scatter(fsend, frecv, fr_s)
+    push(pv, cv, c_s, after)
 
     scol = lax.broadcasted_iota(jnp.int32, (rows, H * HB), 1)
     owner_t = jnp.zeros_like(scol)
@@ -176,15 +167,15 @@
     hot = lax.broadcasted_iota(jnp.int32, s0.shape, 0) == pos_ref[...]
     spos = jnp.sum(jnp.where(hot, s0, 0.0), axis=0, keepdims=True)
 
-    arrive(f1)
+    arrive(frecv, fr_s)
     fx[...] = (load_part(fsend) + jnp.sum(frecv[...].astype(jnp.float32), axis=0)).astype(jnp.bfloat16)
-    f2 = middle(fx, fxr, fx_s)
-    arrive(f2)
+    middle(fx, fxr, fx_s)
+    arrive(fxr, fx_s)
     part(hv, z)[...] = (
         fx[...].astype(jnp.float32) + jnp.sum(fxr[...].astype(jnp.float32), axis=0)
     ).astype(jnp.bfloat16)
-    f3 = gather(hv, fa_s)
-    cyc.wait_recv()
+    gather(hv, fa_s)
+    arrive(cv, c_s)
     s1 = nt(cv[...], q) * scale
     top01 = jnp.maximum(jnp.max(s0, axis=0, keepdims=True), jnp.max(s1, axis=0, keepdims=True))
     sum01 = jnp.sum(jnp.exp(s0 - top01), axis=0, keepdims=True) + jnp.sum(
@@ -195,7 +186,7 @@
     first = jnp.where(lane < GQ, pick_ref[0:1, 0:1], pick_ref[1:2, 0:1])
     second = jnp.where(lane < GQ, pick_ref[0:1, 1:2], pick_ref[1:2, 1:2])
     picked = (slot == first) | (slot == second)
-    arrive(f3)
+    arrive(frecv, fa_s)
     s2 = nt(hv[...], q) * scale
 
     s2 = jnp.where(picked, s2, -jnp.inf)
@@ -203,45 +194,54 @@
     total = sum01 * jnp.exp(top01 - top) + jnp.sum(jnp.exp(s2 - top), axis=0, keepdims=True)
     lse = top + jnp.log(total)
 
-    forward = list(sent)
-    sent.clear()
     g2 = jnp.exp(s2 - lse).astype(jnp.bfloat16)
     gsend[...] = (nn(g2, q) * scale).astype(jnp.bfloat16)
-    b1 = scatter(gsend, grecv, gr_s)
+    scatter(gsend, grecv, gr_s)
 
     l1[...] = lse - spos
-    a1 = [push(l1, l1r.at[d - 1], ss.at[next(sends)], l1_s.at[d - 1], zpeer[d]) for d in ZORDER]
+    for d in ZORDER:
+        push(l1, l1r.at[d - 1], l1_s, zpeer[d])
 
     g1 = jnp.exp(s1 - lse).astype(jnp.bfloat16)
     cgs[...] = (nn(g1, q) * scale).astype(jnp.bfloat16)
-    back = push(cgs, cgr, ss.at[next(sends)], c_s.at[1], before)
+    push(cgs, cgr, k_s, before)
 
     g0 = (jnp.exp(s0 - lse) - hot.astype(jnp.float32)).astype(jnp.bfloat16)
     og[...] = nn(g0, q) * scale
     out_ref[0] = ((tn(g0, pv[...]) + tn(g1, cv[...]) + tn(g2, hv[...])) * scale).astype(jnp.bfloat16)
 
-    for copy in forward:
-        copy.wait_send()
-    arrive(b1)
+    leave(frecv, fr_s)
+    leave(fxr, fx_s)
+    leave(frecv, fa_s)
+    leave(cv, c_s)
+    arrive(grecv, gr_s)
     gx[...] = (load_part(gsend) + jnp.sum(grecv[...].astype(jnp.float32), axis=0)).astype(jnp.bfloat16)
-    b2 = middle(gx, gxr, gx_s)
-    arrive(a1)
+    middle(gx, gxr, gx_s)
+    arrive(l1r, l1_s)
     l2[...] = l1[...] + jnp.sum(l1r[...], axis=0)
-    a2 = [push(l2, l2r.at[d - 1], ss.at[next(sends)], l2_s.at[d - 1], ypeer[d]) for d in ZORDER]
-    arrive(b2)
+    for d in ZORDER:
+        push(l2, l2r.at[d - 1], l2_s, ypeer[d])
+    arrive(gxr, gx_s)
     part(gt, z)[...] = (
         gx[...].astype(jnp.float32) + jnp.sum(gxr[...].astype(jnp.float32), axis=0)
     ).astype(jnp.bfloat16)
-    b3 = gather(gt, ga_s)
-    arrive(a2)
+    gather(gt, ga_s)
+    arrive(l2r, l2_s)
     l3[...] = l2[...] + jnp.sum(l2r[...], axis=0)
-    a3 = [push(l3, l3r.at[d - 1], ss.at[next(sends)], l3_s.at[d - 1], xpeer[d]) for d in range(1, 8)]
-    back.wait_recv()
+    for d in range(1, 8):
+        push(l3, l3r.at[d - 1], l3_s, xpeer[d])
+    arrive(cgr, k_s)
     og[...] += cgr[...].astype(jnp.float32)
-    arrive(a3)
+    arrive(l3r, l3_s)
     loss_ref[0, 0] = jnp.sum(l3[...] + jnp.sum(l3r[...], axis=0)) / n_all
-    leave()
-    arrive(b3)
+    leave(grecv, gr_s)
+    leave(gxr, gx_s)
+    leave(grecv, ga_s)
+    leave(cgr, k_s)
+    leave(l1r, l1_s)
+    leave(l2r, l2_s)
+    leave(l3r, l3_s)
+    arrive(grecv, ga_s)
     out_ref[1] = (og[...] + nn(sel_t, gt[...])).astype(jnp.bfloat16)
 
 
@@ -291,17 +291,17 @@
             pltpu.VMEM((1, rows), f32),
             pltpu.VMEM((7, 1, rows), f32),
             dma((6,)),
-            dma((64,)),
-            dma((NZ - 1,)),
-            dma((3,)),
-            dma((NZ - 1,)),
-            dma((NZ - 1,)),
-            dma((3,)),
-            dma((NZ - 1,)),
-            dma((2,)),
-            dma((7,)),
-            dma((7,)),
-            dma((7,)),
+            dma((2,)),
+            dma((2,)),
+            dma((2,)),
+            dma((2,)),
+            dma((2,)),
+            dma((2,)),
+            dma((2,)),
+            dma((2,)),
+            dma((2,)),
+            dma((2,)),
+            dma((2,)),
         ],
         compiler_params=pltpu.CompilerParams(collective_id=0, has_side_effects=True),
         name="retriever",

time: 47.6 us -> 46.6 us (0.979)
  Pallas kernels: 45.5 us -> 44.5 us
    pallas_call x1, Pallas kernels: 45.5 us -> 44.5 us  [body(): pl.pallas_call(functools.partial(kernel, n_all), out_shape=(pltpu.SMEM((1...]
where the time goes in v5:
time: 46.6 us; the launch traced here: 46.5 us
  Pallas kernels  44.5 us (95%)
  between operations  1.16 us (2%)
  local copies, waits for them, and re-layouts  0.77 us (2%)
    pallas_call x1, Pallas kernels, body(): pl.pallas_call(functools.partial(kernel, n_all), out_shape=(pltpu.SMEM((1...  44.5 us

profile of v5, /device:TPU:1, one launch (start us, length us, event | category | flops | bytes accessed | tf_op | source)
XLA Modules:
  0.0 46.5 jit_solution(7758243392047470287)
XLA Ops:
  0.6 44.5 %retriever.1 = (f32[1,1]{1,0:T(1,128)S(4)}, bf16[2,128,768]{2,1,0:T(8,128)(2,1)S(1)}) custom-call(bf16[128,768]{1,0:T(8,128)(2,1)} %q_hbm.1, bf16[128,768]{1,0:T(8,128)(2,1)} %p_hbm.1, s32[1,128]{1,0:T(1,128)} %bitcast.6, s32[1,4]{1,0:T(1,128)} %own_hbm.1, s32[1,4]{1,0:T(1,128)} %blk_hbm.1, s32[2,2]{1,0:T(2,128)} %pick_hbm.1), custom_call_target="tpu_custom_call" | custom-call | tf_op jit(solution)/shard_map/retriever/pallas_call | solution.py:258
  45.7 0.8 %slice_bitcast_fusion = (bf16[128,768]{1,0:T(8,128)(2,1)}, bf16[128,768]{1,0:T(8,128)(2,1)}) fusion(bf16[2,128,768]{2,1,0:T(8,128)(2,1)S(1)} %get-tuple-element.6), kind=kLoop, calls=%fused_computation | loop fusion | bytes 786432 | tf_op jit(solution)/shard_map/squeeze | solution.py:309

commit v6 on v5

--- a/solution.py
+++ b/solution.py
@@ -11,14 +11,11 @@
 H = 4
 HB = 16
 GQ = 64
+SHARED = H * HB
 NZ = 8
 NX = 4
 NYL = 4
 ZORDER = (4, 3, 5, 2, 6, 1, 7)
-
-
-def nt(a, b):
-    return lax.dot_general(a, b, (((1,), (1,)), ((), ())), preferred_element_type=jnp.float32)
 
 
 def nn(a, b):
@@ -34,7 +31,7 @@
     q_hbm, p_hbm, pos_hbm, own_hbm, blk_hbm, pick_hbm,
     loss_ref, out_ref,
     pos_ref, own_ref, blk_ref, pick_ref,
-    qv, pv, cv, hv, fsend, frecv, fx, fxr,
+    qt, qv, pv, cv, hv, fsend, frecv, fx, fxr,
     gsend, grecv, gx, gxr, gt, cgs, cgr, og,
     l1, l1r, l2, l2r, l3, l3r,
     lsem, fr_s, fx_s, fa_s, gr_s, gx_s, ga_s, c_s, k_s, l1_s, l2_s, l3_s,
@@ -44,33 +41,32 @@
     rows, width = p_hbm.shape
     scale = width ** (-0.5)
     half = width // 2
-    z = neg // 4
-    yh = (neg // 2) % 2
-    core = neg % 2
-    x = blk // NYL
-    yl = blk % NYL
+    z = lax.div(neg, 4)
+    yc = lax.rem(neg, 4)
+    yh = lax.div(yc, 2)
+    core = lax.rem(yc, 2)
+    x = lax.div(blk, NYL)
+    yl = lax.rem(blk, NYL)
     y = yh * NYL + yl
-
-    zpeer = {d: {"blk": blk, "neg": ((z + d) % NZ) * 4 + yh * 2 + core} for d in range(1, NZ)}
-    ypeer = {
-        d: {
-            "blk": x * NYL + ((y + d) % 8) % NYL,
-            "neg": z * 4 + (((y + d) % 8) // NYL) * 2 + core,
-        }
-        for d in range(1, 8)
+    zbase = z * 4
+
+    zat = {d: lax.rem(z + d, NZ) for d in range(1, NZ)}
+    zpeer = {d: {"blk": blk, "neg": zat[d] * 4 + yc} for d in range(1, NZ)}
+    mpeer = {
+        1: {"blk": blk, "neg": zbase + yh * 2 + (1 - core)},
+        2: {"blk": blk, "neg": zbase + (1 - yh) * 2 + core},
+        3: {"blk": blk, "neg": zbase + (1 - yh) * 2 + (1 - core)},
     }
+    after = {"blk": lax.rem(blk + 1, 16), "neg": neg}
+    before = {"blk": lax.rem(blk + 15, 16), "neg": neg}
+    ypeer = {}
+    for d in range(1, 8):
+        yd = lax.rem(y + d, 8)
+        ypeer[d] = {"blk": x * NYL + lax.rem(yd, NYL), "neg": zbase + lax.div(yd, NYL) * 2 + core}
     xpeer = {}
     for d in range(1, 8):
-        xpeer[d] = {
-            "blk": ((x + d // 2) % NX) * NYL + yl,
-            "neg": z * 4 + yh * 2 + (core + d % 2) % 2,
-        }
-    mpeer = {
-        d: {"blk": blk, "neg": z * 4 + ((yh + d // 2) % 2) * 2 + (core + d % 2) % 2}
-        for d in range(1, 4)
-    }
-    after = {"blk": (blk + 1) % 16, "neg": neg}
-    before = {"blk": (blk + 15) % 16, "neg": neg}
+        xd = lax.rem(x + d // 2, NX)
+        xpeer[d] = {"blk": xd * NYL + yl, "neg": mpeer[1]["neg"] if d % 2 else neg}
 
     load_p = pltpu.make_async_copy(p_hbm, pv, lsem.at[0])
     load_q = pltpu.make_async_copy(q_hbm, qv, lsem.at[1])
@@ -104,7 +100,8 @@
     chosen = (owner == neg) & (place * HB + srow % HB == lax.broadcasted_iota(jnp.int32, srow.shape, 1))
     sel = chosen.astype(jnp.float32).astype(jnp.bfloat16)
     load_p.wait()
-    fsend[...] = nn(sel, pv[...]).astype(jnp.bfloat16)
+    fsend[0:SHARED, :] = nn(sel, pv[:, :half]).astype(jnp.bfloat16)
+    fsend[SHARED:, :] = nn(sel, pv[:, half:]).astype(jnp.bfloat16)
     pl.semaphore_wait(barrier, len(greet))
 
     def push(src, dst, sems, who):
@@ -126,14 +123,11 @@
         all_of(ref, sems).wait_send()
 
     def part(ref, index):
-        return ref.at[
-            pl.ds(pl.multiple_of((index // 2) * HB, HB), HB),
-            pl.ds(pl.multiple_of((index % 2) * half, half), half),
-        ]
+        return ref.at[pl.ds(pl.multiple_of(index * HB, HB), HB), :]
 
     def scatter(buf, land, sems):
         for d in ZORDER:
-            push(part(buf, (z + d) % NZ), land.at[d - 1], sems, zpeer[d])
+            push(part(buf, zat[d]), land.at[d - 1], sems, zpeer[d])
 
     def gather(buf, sems):
         for d in ZORDER:
@@ -163,7 +157,8 @@
     load_pos.wait()
     load_pick.wait()
     q = qv[...]
-    s0 = nt(pv[...], q) * scale
+    qt[...] = q.T
+    s0 = nn(pv[...], qt[...]) * scale
     hot = lax.broadcasted_iota(jnp.int32, s0.shape, 0) == pos_ref[...]
     spos = jnp.sum(jnp.where(hot, s0, 0.0), axis=0, keepdims=True)
 
@@ -176,7 +171,7 @@
     ).astype(jnp.bfloat16)
     gather(hv, fa_s)
     arrive(cv, c_s)
-    s1 = nt(cv[...], q) * scale
+    s1 = nn(cv[...], qt[...]) * scale
     top01 = jnp.maximum(jnp.max(s0, axis=0, keepdims=True), jnp.max(s1, axis=0, keepdims=True))
     sum01 = jnp.sum(jnp.exp(s0 - top01), axis=0, keepdims=True) + jnp.sum(
         jnp.exp(s1 - top01), axis=0, keepdims=True
@@ -187,7 +182,7 @@
     second = jnp.where(lane < GQ, pick_ref[0:1, 1:2], pick_ref[1:2, 1:2])
     picked = (slot == first) | (slot == second)
     arrive(frecv, fa_s)
-    s2 = nt(hv[...], q) * scale
+    s2 = (nn(hv[0:SHARED, :], qt[:half, :]) + nn(hv[SHARED:, :], qt[half:, :])) * scale
 
     s2 = jnp.where(picked, s2, -jnp.inf)
     top = jnp.maximum(top01, jnp.max(s2, axis=0, keepdims=True))
@@ -195,7 +190,8 @@
     lse = top + jnp.log(total)
 
     g2 = jnp.exp(s2 - lse).astype(jnp.bfloat16)
-    gsend[...] = (nn(g2, q) * scale).astype(jnp.bfloat16)
+    gsend[0:SHARED, :] = (nn(g2, q[:, :half]) * scale).astype(jnp.bfloat16)
+    gsend[SHARED:, :] = (nn(g2, q[:, half:]) * scale).astype(jnp.bfloat16)
     scatter(gsend, grecv, gr_s)
 
     l1[...] = lse - spos
@@ -208,7 +204,15 @@
 
     g0 = (jnp.exp(s0 - lse) - hot.astype(jnp.float32)).astype(jnp.bfloat16)
     og[...] = nn(g0, q) * scale
-    out_ref[0] = ((tn(g0, pv[...]) + tn(g1, cv[...]) + tn(g2, hv[...])) * scale).astype(jnp.bfloat16)
+    for side, lo in ((0, 0), (1, half)):
+        out_ref[0, :, lo:lo + half] = (
+            (
+                tn(g0, pv[:, lo:lo + half])
+                + tn(g1, cv[:, lo:lo + half])
+                + tn(g2, hv[side * SHARED:(side + 1) * SHARED, :])
+            )
+            * scale
+        ).astype(jnp.bfloat16)
 
     leave(frecv, fr_s)
     leave(fxr, fx_s)
@@ -242,7 +246,9 @@
     leave(l2r, l2_s)
     leave(l3r, l3_s)
     arrive(grecv, ga_s)
-    out_ref[1] = (og[...] + nn(sel_t, gt[...])).astype(jnp.bfloat16)
+    for side, lo in ((0, 0), (1, half)):
+        shared = gt[side * SHARED:(side + 1) * SHARED, :]
+        out_ref[1, :, lo:lo + half] = (og[:, lo:lo + half] + nn(sel_t, shared)).astype(jnp.bfloat16)
 
 
 def body(queries, passages, positive, hard_owner, hard_block, hard_pick):
@@ -268,19 +274,20 @@
             pltpu.VMEM(hard_owner.shape, jnp.int32),
             pltpu.VMEM(hard_block.shape, jnp.int32),
             pltpu.VMEM(hard_pick.shape, jnp.int32),
-            pltpu.VMEM((rows, width), bf),
-            pltpu.VMEM((rows, width), bf),
-            pltpu.VMEM((rows, width), bf),
-            pltpu.VMEM((H * HB, width), bf),
-            pltpu.VMEM((H * HB, width), bf),
+            pltpu.VMEM((width, rows), bf),
+            pltpu.VMEM((rows, width), bf),
+            pltpu.VMEM((rows, width), bf),
+            pltpu.VMEM((rows, width), bf),
+            pltpu.VMEM((2 * SHARED, half), bf),
+            pltpu.VMEM((2 * SHARED, half), bf),
             pltpu.VMEM((NZ - 1, HB, half), bf),
             pltpu.VMEM((HB, half), bf),
             pltpu.VMEM((3, HB, half), bf),
-            pltpu.VMEM((H * HB, width), bf),
+            pltpu.VMEM((2 * SHARED, half), bf),
             pltpu.VMEM((NZ - 1, HB, half), bf),
             pltpu.VMEM((HB, half), bf),
             pltpu.VMEM((3, HB, half), bf),
-            pltpu.VMEM((H * HB, width), bf),
+            pltpu.VMEM((2 * SHARED, half), bf),
             pltpu.VMEM((rows, width), bf),
             pltpu.VMEM((rows, width), bf),
             pltpu.VMEM((rows, width), f32),

time: 46.6 us -> 46.5 us (level)
  no operation moved by 1% of the time
where the time goes in v6:
time: 46.5 us; the launch traced here: 46.3 us
  Pallas kernels  44.4 us (95%)
  between operations  1.16 us (2%)
  local copies, waits for them, and re-layouts  0.77 us (2%)
    pallas_call x1, Pallas kernels, body(): pl.pallas_call(functools.partial(kernel, n_all), out_shape=(pltpu.SMEM((1...  44.4 us

profile of v6, /device:TPU:1, one launch (start us, length us, event | category | flops | bytes accessed | tf_op | source)
XLA Modules:
  0.0 46.3 jit_solution(16010175026079364689)
XLA Ops:
  0.6 44.4 %retriever.1 = (f32[1,1]{1,0:T(1,128)S(4)}, bf16[2,128,768]{2,1,0:T(8,128)(2,1)S(1)}) custom-call(bf16[128,768]{1,0:T(8,128)(2,1)} %q_hbm.1, bf16[128,768]{1,0:T(8,128)(2,1)} %p_hbm.1, s32[1,128]{1,0:T(1,128)} %bitcast.6, s32[1,4]{1,0:T(1,128)} %own_hbm.1, s32[1,4]{1,0:T(1,128)} %blk_hbm.1, s32[2,2]{1,0:T(2,128)} %pick_hbm.1), custom_call_target="tpu_custom_call" | custom-call | tf_op jit(solution)/shard_map/retriever/pallas_call | solution.py:264
  45.6 0.8 %slice_bitcast_fusion = (bf16[128,768]{1,0:T(8,128)(2,1)}, bf16[128,768]{1,0:T(8,128)(2,1)}) fusion(bf16[2,128,768]{2,1,0:T(8,128)(2,1)S(1)} %get-tuple-element.6), kind=kLoop, calls=%fused_computation | loop fusion | bytes 786432 | tf_op jit(solution)/shard_map/squeeze | solution.py:316

commit v7 on v6

--- a/solution.py
+++ b/solution.py
@@ -68,13 +68,15 @@
         xd = lax.rem(x + d // 2, NX)
         xpeer[d] = {"blk": xd * NYL + yl, "neg": mpeer[1]["neg"] if d % 2 else neg}
 
-    load_p = pltpu.make_async_copy(p_hbm, pv, lsem.at[0])
+    load_p = pltpu.make_async_copy(p_hbm.at[:, pl.ds(0, half)], pv.at[:, pl.ds(0, half)], lsem.at[0])
+    load_r = pltpu.make_async_copy(p_hbm.at[:, pl.ds(half, half)], pv.at[:, pl.ds(half, half)], lsem.at[6])
     load_q = pltpu.make_async_copy(q_hbm, qv, lsem.at[1])
     load_own = pltpu.make_async_copy(own_hbm, own_ref, lsem.at[2])
     load_blk = pltpu.make_async_copy(blk_hbm, blk_ref, lsem.at[3])
     load_pos = pltpu.make_async_copy(pos_hbm, pos_ref, lsem.at[4])
     load_pick = pltpu.make_async_copy(pick_hbm, pick_ref, lsem.at[5])
     load_p.start()
+    load_r.start()
 
     barrier = pltpu.get_barrier_semaphore()
     greet = [zpeer[4], mpeer[3], ypeer[4], after, before]
@@ -101,6 +103,7 @@
     sel = chosen.astype(jnp.float32).astype(jnp.bfloat16)
     load_p.wait()
     fsend[0:SHARED, :] = nn(sel, pv[:, :half]).astype(jnp.bfloat16)
+    load_r.wait()
     fsend[SHARED:, :] = nn(sel, pv[:, half:]).astype(jnp.bfloat16)
     pl.semaphore_wait(barrier, len(greet))
 
@@ -163,7 +166,7 @@
     spos = jnp.sum(jnp.where(hot, s0, 0.0), axis=0, keepdims=True)
 
     arrive(frecv, fr_s)
-    fx[...] = (load_part(fsend) + jnp.sum(frecv[...].astype(jnp.float32), axis=0)).astype(jnp.bfloat16)
+    fx[...] = part(fsend, z)[...] + sum(frecv[i] for i in range(NZ - 1))
     middle(fx, fxr, fx_s)
     arrive(fxr, fx_s)
     part(hv, z)[...] = (
@@ -297,7 +300,7 @@
             pltpu.VMEM((7, 1, rows), f32),
             pltpu.VMEM((1, rows), f32),
             pltpu.VMEM((7, 1, rows), f32),
-            dma((6,)),
+            dma((7,)),
             dma((2,)),
             dma((2,)),
             dma((2,)),

time: 46.5 us -> 46.5 us (level)
  no operation moved by 1% of the time
where the time goes in v7:
time: 46.5 us; the launch traced here: 46.3 us
  Pallas kernels  44.4 us (95%)
  between operations  1.16 us (2%)
  local copies, waits for them, and re-layouts  0.77 us (2%)
    pallas_call x1, Pallas kernels, body(): pl.pallas_call(functools.partial(kernel, n_all), out_shape=(pltpu.SMEM((1...  44.4 us

profile of v7, /device:TPU:1, one launch (start us, length us, event | category | flops | bytes accessed | tf_op | source)
XLA Modules:
  0.0 46.3 jit_solution(13703912378779453109)
XLA Ops:
  0.6 44.4 %retriever.1 = (f32[1,1]{1,0:T(1,128)S(4)}, bf16[2,128,768]{2,1,0:T(8,128)(2,1)S(1)}) custom-call(bf16[128,768]{1,0:T(8,128)(2,1)} %q_hbm.1, bf16[128,768]{1,0:T(8,128)(2,1)} %p_hbm.1, s32[1,128]{1,0:T(1,128)} %bitcast.6, s32[1,4]{1,0:T(1,128)} %own_hbm.1, s32[1,4]{1,0:T(1,128)} %blk_hbm.1, s32[2,2]{1,0:T(2,128)} %pick_hbm.1), custom_call_target="tpu_custom_call" | custom-call | tf_op jit(solution)/shard_map/retriever/pallas_call | solution.py:267
  45.6 0.8 %slice_bitcast_fusion = (bf16[128,768]{1,0:T(8,128)(2,1)}, bf16[128,768]{1,0:T(8,128)(2,1)}) fusion(bf16[2,128,768]{2,1,0:T(8,128)(2,1)S(1)} %get-tuple-element.6), kind=kLoop, calls=%fused_computation | loop fusion | bytes 786432 | tf_op jit(solution)/shard_map/squeeze | solution.py:319
